TPU v7x, 32 devices: a whole 2x2x4 slice. The times are simulated.
32 devices in a mesh: seq: 16 (over z, y, x), head: 2 (over core).
Axes of the slice: x: 2, y: 2, z: 4, core: 2. Of those that a mesh axis runs over, the one named last changes fastest.
Arguments:
- tokens: bfloat16 [2, 4096, 2048], P(None, 'seq'), may hold values from -6 to 6
- grad_out: bfloat16 [2, 4096, 2048], P(None, 'seq'), may hold values from -6 to 6
- query_weight: bfloat16 [2048, 2048], P('seq', 'head'), may hold values from -0.5 to 0.5
- key_weight: bfloat16 [2048, 2048], P('seq', 'head'), may hold values from -0.5 to 0.5
- value_weight: bfloat16 [2048, 2048], P('seq', 'head'), may hold values from -0.125 to 0.125
- forget_weight: bfloat16 [2048, 256], P('seq', 'head'), may hold values from -0.125 to 0.125
- forget_bias: bfloat16 [4, 64], P('head', 'seq'), as said below
- outgate_weight: bfloat16 [2048, 2048], P('seq', 'head'), may hold values from -0.125 to 0.125
- output_weight: bfloat16 [2048, 2048], P('head', 'seq'), may hold values from -0.125 to 0.125
- slot_gain: bfloat16 [512], P('seq'), may hold values from 0.5 to 1.5
- first_gain: bfloat16 [2048], P('seq'), may hold values from 0.5 to 1.5
- second_gain: bfloat16 [2048], P('seq'), may hold values from 0.5 to 1.5
- gate_weight: bfloat16 [2048, 5632], P('seq', 'head'), may hold values from -0.125 to 0.125
- up_weight: bfloat16 [2048, 5632], P('seq', 'head'), may hold values from -0.125 to 0.125
- down_weight: bfloat16 [5632, 2048], P('head', 'seq'), may hold values from -0.078125 to 0.078125
Outputs:
- output: bfloat16 [2, 4096, 2048], P(None, 'seq')
- input_grad: float32 [2, 4096, 2048], P(None, 'seq')
- query_grad: float32 [2048, 2048], P('seq', 'head')
- key_grad: float32 [2048, 2048], P('seq', 'head')
- value_grad: float32 [2048, 2048], P('seq', 'head')
- forget_grad: float32 [2048, 256], P('seq', 'head')
- forget_bias_grad: float32 [4, 64], P('head', 'seq')
- outgate_grad: float32 [2048, 2048], P('seq', 'head')
- output_grad: float32 [2048, 2048], P('head', 'seq')
- slot_gain_grad: float32 [512], P('seq')
- first_gain_grad: float32 [2048], P('seq')
- second_gain_grad: float32 [2048], P('seq')
- gate_grad: float32 [2048, 5632], P('seq', 'head')
- up_grad: float32 [2048, 5632], P('seq', 'head')
- down_grad: float32 [5632, 2048], P('head', 'seq')
Inputs may be any that keep to these rules, and one draw needn't show every extreme that they name: `forget_bias`: forget gate offsets of the heads and slots, those of per-token decay rates between 0.25 / 4096 and 1 / 30, so about 1 to 9.
All inputs are finite; a program needn't handle non-finite values.
Results may differ from a plain program's by a relative error of at most 0.01655.
Values may be sent and summed in bfloat16 or wider, within the bound.
A program may use at most 320 MiB of HBM per device.

v0:
```python
import jax
import jax.numpy as jnp
from jax import lax
from jax.sharding import PartitionSpec as P

HIGH = lax.Precision.HIGHEST
TAU = 8.0
EPS = 1e-06


def prefix_2(shard, axis, combine, identity):
    size, here = (lax.axis_size(axis), lax.axis_index(axis))
    everything = jax.tree.map(lambda part: lax.all_gather(part, axis), shard)
    start = jax.tree.map(
        lambda part, zero: jnp.broadcast_to(jnp.asarray(zero, part.dtype), part.shape),
        shard,
        identity,
    )

    def prefix_hop(k, before):
        reached = k < here
        new = combine(before, jax.tree.map(lambda part: part[k], everything))
        return jax.tree.map(lambda a, b: jnp.where(reached, a, b), new, before)

    return lax.fori_loop(0, size, prefix_hop, start)


def entering(shard, axis, combine, identity):
    size, here = (lax.axis_size(axis), lax.axis_index(axis))
    everything = jax.tree.map(
        lambda part, kind: lax.all_gather(part.astype(kind), axis),
        shard,
        jax.tree.map(lambda a: jnp.bfloat16 if a.dtype == jnp.float32 else a.dtype, shard),
    )
    start = jax.tree.map(
        lambda part, zero: jnp.broadcast_to(jnp.asarray(zero, part.dtype), part.shape),
        shard,
        identity,
    )

    def entering_hop(k, before):
        at = size - 1 - k
        reached = at > here
        new = combine(
            before, jax.tree.map(lambda part, own: part[at].astype(own.dtype), everything, shard)
        )
        return jax.tree.map(lambda a, b: jnp.where(reached, a, b), new, before)

    return lax.fori_loop(0, size, entering_hop, start)


def rms_scale(values, gain):
    return values * lax.rsqrt(jnp.mean(values * values, axis=-1, keepdims=True) + EPS) * gain


def out_gate(attended, gate, gain):
    return rms_scale(attended, gain) * jax.nn.silu(gate)


def swiglu(ff_gate, ff_up):
    return jax.nn.silu(ff_gate) * ff_up


def silu_slope(values):
    sig = jax.nn.sigmoid(values)
    return sig + values * sig * (1.0 - sig)


def slot_single(query, keys, values, log_decay, keys_in, values_in):
    count = query.shape[0]
    keep = -jnp.expm1(log_decay)
    total = jnp.cumsum(log_decay, axis=0)
    causal = (jnp.arange(count)[:, None] >= jnp.arange(count)[None, :])[:, :, None]
    spread = jnp.where(causal, total[:, None, :] - total[None, :, :], 0.0)
    mixing = jnp.where(causal, jnp.exp(spread), 0.0) * keep[None, :, :]
    scaled = query * query.shape[1] ** (-0.5)
    paired = jnp.dot(scaled, keys.T, precision=HIGH)
    growth = jnp.exp(total)
    scores = jnp.einsum("ts,tsi->ti", paired, mixing, precision=HIGH) + growth * jnp.dot(
        scaled, keys_in.T, precision=HIGH
    )
    probs = jax.nn.softmax(scores, axis=-1)
    weights = jnp.einsum("ti,tsi->ts", probs, mixing, precision=HIGH)
    return jnp.dot(weights, values, precision=HIGH) + jnp.dot(
        probs * growth, values_in, precision=HIGH
    )


def slot_end(keys, values, log_decay):
    total = jnp.cumsum(log_decay, axis=0)
    last = total[-1]
    weight = jnp.exp(last[None, :] - total) * -jnp.expm1(log_decay)
    return (
        jnp.exp(last),
        jnp.dot(weight.T, keys, precision=HIGH),
        jnp.dot(weight.T, values, precision=HIGH),
    )


def heads_attend(query, keys, values, log_decay, keys_in, values_in):

    def one_head(parts):
        return jax.vmap(slot_single)(parts[0], parts[1], parts[2], parts[3], parts[4], parts[5])

    stacked = (
        jnp.moveaxis(query, 2, 0),
        jnp.moveaxis(keys, 2, 0),
        jnp.moveaxis(values, 2, 0),
        jnp.moveaxis(log_decay, 2, 0),
        jnp.moveaxis(keys_in, 1, 0),
        jnp.moveaxis(values_in, 1, 0),
    )
    return jnp.moveaxis(lax.map(jax.checkpoint(one_head), stacked), 0, 2)


def heads_end(keys, values, log_decay):
    inner = jax.vmap(slot_end, in_axes=(1, 1, 1), out_axes=0)
    return jax.vmap(inner, in_axes=(0, 0, 0), out_axes=0)(keys, values, log_decay)


def carry_combine(earlier, later):
    return (
        earlier[0] * later[0],
        later[1] + later[0][..., None] * earlier[1],
        later[2] + later[0][..., None] * earlier[2],
    )


def matmul(left, right):
    return jnp.dot(left, right, preferred_element_type=jnp.float32)


def outer_sum(left, right):
    return jnp.einsum("bti,btj->ij", left, right, preferred_element_type=jnp.float32)


def back_product(grad, weight):
    return jnp.einsum("btj,ij->bti", grad, weight, preferred_element_type=jnp.float32)


def shards(
    tokens,
    grad_out,
    query_weight,
    key_weight,
    value_weight,
    forget_weight,
    forget_bias,
    outgate_weight,
    output_weight,
    slot_gain,
    first_gain,
    second_gain,
    gate_weight,
    up_weight,
    down_weight,
):
    full = (
        lax.all_gather(query_weight, "seq", axis=0, tiled=True),
        lax.all_gather(key_weight, "seq", axis=0, tiled=True),
        lax.all_gather(value_weight, "seq", axis=0, tiled=True),
        lax.all_gather(forget_weight, "seq", axis=0, tiled=True),
        lax.all_gather(forget_bias, "seq", axis=1, tiled=True),
        lax.all_gather(outgate_weight, "seq", axis=0, tiled=True),
        lax.all_gather(output_weight, "seq", axis=1, tiled=True),
        lax.all_gather(slot_gain, "seq", axis=0, tiled=True),
        lax.all_gather(first_gain, "seq", axis=0, tiled=True),
        lax.all_gather(second_gain, "seq", axis=0, tiled=True),
        lax.all_gather(gate_weight, "seq", axis=0, tiled=True),
        lax.all_gather(up_weight, "seq", axis=0, tiled=True),
        lax.all_gather(down_weight, "seq", axis=1, tiled=True),
    )
    query_full = full[0]
    key_full = full[1]
    value_full = full[2]
    forget_full = full[3]
    bias_full = full[4]
    outgate_full = full[5]
    output_full = full[6]
    slot_full = full[7]
    first_full = full[8]
    second_full = full[9]
    gate_full = full[10]
    up_full = full[11]
    down_full = full[12]
    seqs = tokens.shape[0]
    rows = tokens.shape[1]
    heads_here = bias_full.shape[0]
    slots = bias_full.shape[1]
    head_dim = slot_full.shape[0]

    def split_heads(array, inner):
        return array.reshape(seqs, rows, heads_here, inner)

    def join_heads(array):
        return array.reshape(seqs, rows, heads_here * array.shape[3])

    inputs = tokens.astype(jnp.float32)
    normed_one, first_back = jax.vjp(rms_scale, inputs, first_full.astype(jnp.float32))
    normed_one_low = normed_one.astype(jnp.bfloat16)
    query_low = matmul(normed_one_low, query_full).astype(jnp.bfloat16)
    key_low = matmul(normed_one_low, key_full).astype(jnp.bfloat16)
    value_low = matmul(normed_one_low, value_full).astype(jnp.bfloat16)
    forget_logit = matmul(normed_one_low, forget_full) + bias_full.astype(jnp.float32).reshape(
        heads_here * slots
    )
    outgate_pre = matmul(normed_one_low, outgate_full)
    log_decay = split_heads(-jax.nn.softplus(-forget_logit) / TAU, slots)
    query_wide = split_heads(query_low.astype(jnp.float32), head_dim)
    key_wide = split_heads(key_low.astype(jnp.float32), head_dim)
    value_wide = split_heads(value_low.astype(jnp.float32), head_dim)
    query_feat = jax.nn.silu(query_wide)
    key_feat = jax.nn.silu(key_wide)
    decay, local_keys, local_values = heads_end(key_feat, value_wide, log_decay)
    prefix = prefix_2(
        (decay, local_keys, local_values),
        "seq",
        carry_combine,
        (jnp.ones_like(decay), jnp.zeros_like(local_keys), jnp.zeros_like(local_values)),
    )
    keys_in = prefix[1]
    values_in = prefix[2]
    attended, attend_back = jax.vjp(
        heads_attend, query_feat, key_feat, value_wide, log_decay, keys_in, values_in
    )
    gated, gate_back = jax.vjp(
        out_gate, attended, split_heads(outgate_pre, head_dim), slot_full.astype(jnp.float32)
    )
    gated_low = join_heads(gated).astype(jnp.bfloat16)
    mixed = lax.psum(matmul(gated_low, output_full), "head")
    residual = inputs + mixed
    normed_two, second_back = jax.vjp(rms_scale, residual, second_full.astype(jnp.float32))
    normed_two_low = normed_two.astype(jnp.bfloat16)
    ff_gate = matmul(normed_two_low, gate_full)
    ff_up = matmul(normed_two_low, up_full)
    activated_wide, swiglu_back = jax.vjp(swiglu, ff_gate, ff_up)
    activated = activated_wide.astype(jnp.bfloat16)
    ff_out = lax.psum(matmul(activated, down_full).astype(jnp.bfloat16), "head").astype(jnp.float32)
    output = (residual + ff_out).astype(jnp.bfloat16)
    again = (
        lax.all_gather(query_weight, "seq", axis=0, tiled=True),
        lax.all_gather(key_weight, "seq", axis=0, tiled=True),
        lax.all_gather(value_weight, "seq", axis=0, tiled=True),
        lax.all_gather(forget_weight, "seq", axis=0, tiled=True),
        lax.all_gather(forget_bias, "seq", axis=1, tiled=True),
        lax.all_gather(outgate_weight, "seq", axis=0, tiled=True),
        lax.all_gather(output_weight, "seq", axis=1, tiled=True),
        lax.all_gather(slot_gain, "seq", axis=0, tiled=True),
        lax.all_gather(first_gain, "seq", axis=0, tiled=True),
        lax.all_gather(second_gain, "seq", axis=0, tiled=True),
        lax.all_gather(gate_weight, "seq", axis=0, tiled=True),
        lax.all_gather(up_weight, "seq", axis=0, tiled=True),
        lax.all_gather(down_weight, "seq", axis=1, tiled=True),
    )
    query_back = again[0]
    key_back = again[1]
    value_back = again[2]
    forget_back = again[3]
    outgate_back = again[5]
    output_back = again[6]
    gate_back_weight = again[10]
    up_back = again[11]
    down_back = again[12]
    down_grad = outer_sum(activated, grad_out)
    act_grad = back_product(grad_out, down_back)
    gate_wide, up_wide = swiglu_back(act_grad)
    gate_term = gate_wide.astype(jnp.bfloat16)
    up_term = up_wide.astype(jnp.bfloat16)
    gate_grad = outer_sum(normed_two_low, gate_term)
    up_grad = outer_sum(normed_two_low, up_term)
    normed_two_grad = back_product(gate_term, gate_back_weight) + back_product(up_term, up_back)
    normed_two_grad = lax.psum(normed_two_grad.astype(jnp.bfloat16), "head").astype(jnp.float32)
    residual_from_norm, second_gain_grad = second_back(normed_two_grad)
    residual_grad = grad_out.astype(jnp.float32) + residual_from_norm
    residual_low = residual_grad.astype(jnp.bfloat16)
    output_grad = outer_sum(gated_low, residual_low)
    gated_grad = split_heads(back_product(residual_low, output_back), head_dim)
    attended_grad, outgate_wide, slot_gain_grad = gate_back(gated_grad)
    outgate_term = join_heads(outgate_wide).astype(jnp.bfloat16)
    query_part, key_part, value_part, decay_part, keys_in_grad, values_in_grad = attend_back(
        attended_grad
    )
    suffix = entering(
        (decay, keys_in_grad, values_in_grad),
        "seq",
        carry_combine,
        (jnp.ones_like(decay), jnp.zeros_like(keys_in_grad), jnp.zeros_like(values_in_grad)),
    )
    decay_cot = jnp.sum(suffix[1] * keys_in + suffix[2] * values_in, axis=-1)
    ends, end_back = jax.vjp(heads_end, key_feat, value_wide, log_decay)
    key_extra, value_extra, decay_extra = end_back((decay_cot, suffix[1], suffix[2]))
    query_term = join_heads(query_part * silu_slope(query_wide)).astype(jnp.bfloat16)
    key_term = join_heads((key_part + key_extra) * silu_slope(key_wide)).astype(jnp.bfloat16)
    value_term = join_heads(value_part + value_extra).astype(jnp.bfloat16)
    forget_term = (
        join_heads(decay_part + decay_extra) * jax.nn.sigmoid(-forget_logit) / TAU
    ).astype(jnp.bfloat16)
    bias_grad = jnp.sum(forget_term.astype(jnp.float32), axis=(0, 1)).reshape(heads_here, slots)
    query_grad = outer_sum(normed_one_low, query_term)
    key_grad = outer_sum(normed_one_low, key_term)
    value_grad = outer_sum(normed_one_low, value_term)
    forget_grad = outer_sum(normed_one_low, forget_term)
    outgate_grad = outer_sum(normed_one_low, outgate_term)
    normed_one_grad = (
        back_product(query_term, query_back)
        + back_product(key_term, key_back)
        + back_product(value_term, value_back)
        + back_product(forget_term, forget_back)
        + back_product(outgate_term, outgate_back)
    )
    normed_one_grad, slot_gain_grad = (
        lax.psum(normed_one_grad.astype(jnp.bfloat16), "head").astype(jnp.float32),
        lax.psum(slot_gain_grad.astype(jnp.bfloat16), "head").astype(jnp.float32),
    )
    input_from_norm, first_gain_grad = first_back(normed_one_grad)
    input_grad = residual_grad + input_from_norm
    summed = (
        lax.psum_scatter(query_grad, "seq", scatter_dimension=0, tiled=True),
        lax.psum_scatter(key_grad, "seq", scatter_dimension=0, tiled=True),
        lax.psum_scatter(value_grad, "seq", scatter_dimension=0, tiled=True),
        lax.psum_scatter(forget_grad, "seq", scatter_dimension=0, tiled=True),
        lax.psum_scatter(bias_grad, "seq", scatter_dimension=1, tiled=True),
        lax.psum_scatter(outgate_grad, "seq", scatter_dimension=0, tiled=True),
        lax.psum_scatter(output_grad, "seq", scatter_dimension=1, tiled=True),
        lax.psum_scatter(slot_gain_grad, "seq", scatter_dimension=0, tiled=True),
        lax.psum_scatter(first_gain_grad, "seq", scatter_dimension=0, tiled=True),
        lax.psum_scatter(second_gain_grad, "seq", scatter_dimension=0, tiled=True),
        lax.psum_scatter(gate_grad, "seq", scatter_dimension=0, tiled=True),
        lax.psum_scatter(up_grad, "seq", scatter_dimension=0, tiled=True),
        lax.psum_scatter(down_grad, "seq", scatter_dimension=1, tiled=True),
    )
    return (
        output,
        input_grad,
        summed[0],
        summed[1],
        summed[2],
        summed[3],
        summed[4],
        summed[5],
        summed[6],
        summed[7],
        summed[8],
        summed[9],
        summed[10],
        summed[11],
        summed[12],
    )


def solution(mesh):
    return jax.shard_map(
        shards,
        mesh=mesh,
        in_specs=(
            P(None, "seq", None),
            P(None, "seq", None),
            P("seq", "head"),
            P("seq", "head"),
            P("seq", "head"),
            P("seq", "head"),
            P("head", "seq"),
            P("seq", "head"),
            P("head", "seq"),
            P("seq"),
            P("seq"),
            P("seq"),
            P("seq", "head"),
            P("seq", "head"),
            P("head", "seq"),
        ),
        out_specs=(
            P(None, "seq", None),
            P(None, "seq", None),
            P("seq", "head"),
            P("seq", "head"),
            P("seq", "head"),
            P("seq", "head"),
            P("head", "seq"),
            P("seq", "head"),
            P("head", "seq"),
            P("seq"),
            P("seq"),
            P("seq"),
            P("seq", "head"),
            P("seq", "head"),
            P("head", "seq"),
        ),
        check_vma=False,
    )
```

profile of v0, /device:TPU:10, one launch (start us, length us, event | category | flops | bytes accessed | tf_op | source)
XLA Modules:
  0.0 4301.3 jit_solution(4325084734223197280)
XLA Ops:
  40.3 40.7 all-gather.7
  83.5 39.9 all_gather.83
  212.1 39.2 all-gather.1
  274.4 85.9 %all-gather.38.cloned.1.call-done = f32[32,2,64,512]{3,2,1,0:T(8,128)} async-done(((f32[2,2,64,512]{3,2,1,0:T(8,128)}), f32[32,2,64,512]{3,2,1,0:T(8,128)}) %all-gather.38.cloned.1.call-update) | async-done | bytes 8388624 | tf_op jit(solution)/shard_map/all_gather | solution.py:13
  360.3 114.2 %all-gather.40.cloned.1.call-done = f32[32,2,64,512]{3,2,1,0:T(8,128)} async-done(((f32[2,2,64,512]{3,2,1,0:T(8,128)}), f32[32,2,64,512]{3,2,1,0:T(8,128)}) %all-gather.40.cloned.1.call-update) | async-done | bytes 8388624 | tf_op jit(solution)/shard_map/all_gather | solution.py:13
  501.5 167.9 %while.73 = (s32[]{:T(128)}, f32[2,2,256,512]{2,3,0,1:T(8,128)}, f32[2,2,256,512]{3,2,1,0:T(8,128)S(1)}, f32[2,2,256,512]{3,2,1,0:T(8,128)}, f32[2,2,256,64]{2,3...) while((s32[]{:T(128)}, f32[2,2,256,512]{2,3,0,1:T(8,128)}, ...), condition=%wide.region_10.11_spmd.clone.clone, body=%wide.region_5.10_spmd.clone.clone.sunk | while | flops 2287010304 | bytes 27807444 | solution.py:113
  720.5 103.7 %all-gather.36.cloned.1.call-done = bf16[2816,2048]{1,0:T(8,128)(2,1)} async-done(((bf16[2816,128]{1,0:T(8,128)(2,1)}), bf16[2816,2048]{1,0:T(8,128)(2,1)}) %all-gather.36.cloned.1.call-update) | async-done | bytes 11534352 | tf_op jit(solution)/shard_map/all_gather | solution.py:171
  864.4 136.7 %all-gather.34.cloned.1.call-done = bf16[2048,2816]{1,0:T(8,128)(2,1)} async-done(((bf16[128,2816]{1,0:T(8,128)(2,1)}), bf16[2048,2816]{1,0:T(8,128)(2,1)}) %all-gather.34.cloned.1.call-update) | async-done | bytes 11534352 | tf_op jit(solution)/shard_map/all_gather | solution.py:170
  1013.6 131.0 %all-gather.32.cloned.1.call-done = bf16[2048,2816]{1,0:T(8,128)(2,1)} async-done(((bf16[128,2816]{1,0:T(8,128)(2,1)}), bf16[2048,2816]{1,0:T(8,128)(2,1)}) %all-gather.32.cloned.1.call-update) | async-done | bytes 11534352 | tf_op jit(solution)/shard_map/all_gather | solution.py:169
  1228.7 367.7 %while.72 = (s32[]{:T(128)}, f32[2,2,256,512]{2,3,0,1:T(8,128)}, f32[2,2,256,512]{2,3,0,1:T(8,128)}, f32[2,2,256,512]{2,3,0,1:T(8,128)}, f32[2,2,256,64]{2,3,1,0...) while((s32[]{:T(128)}, f32[2,2,256,512]{2,3,0,1:T(8,128)}, ...), condition=%wide.region_29.30_spmd, body=%wide.region_18.29_spmd.sunk | while | flops 5497390080 | bytes 115728032 | solution.py:113
  1249.1 34.8 fusion.380
  1287.6 35.2 fusion.376
  1429.6 34.8 fusion.380
  1468.1 35.4 fusion.376
  1678.0 72.6 %all-gather.44.cloned.1.call-done = bf16[32,2,64,512]{3,2,0,1:T(8,128)(2,1)} async-done(((bf16[2,2,64,512]{3,2,0,1:T(8,128)(2,1)}), bf16[32,2,64,512]{3,2,0,1:T(8,128)(2,1)}) %all-gather.44.cloned.1.call-update) | async-done | bytes 4194320 | tf_op jit(solution)/shard_map/all_gather | solution.py:31
  1912.2 71.2 %all-reduce.6 = (f32[2,64]{1,0:T(2,128)S(1)}, f32[512]{0:T(512)S(1)}, f32[2048]{0:T(1024)S(1)}, f32[2048]{0:T(1024)S(1)}) all-reduce(f32[2,64]{1,0:T(2,128)S(1)} %reshape.331, bf16[512]{0:T(512)(128)(2,1)S(1)} %psum.39, f32[2048]{0:T(1024)S(1)} %get-tuple-element.1070, ...), channel_id=12, replica_groups=mesh['seq'=16,'head'=2] {'seq'}, use_global_device_ids=true, to_apply=%region_43.44.clone | all-reduce | flops 4736 | bytes 36864
  1993.1 121.7 %reduce-scatter.21.cloned.1.call-done = f32[1024,128]{1,0:T(8,128)} async-done(((f32[1024,2048]{1,0:T(8,128)}), f32[1024,128]{1,0:T(8,128)}) %reduce-scatter.21.cloned.1.call-update) | async-done | bytes 524304 | tf_op jit(solution)/shard_map/reduce_scatter | solution.py:324
  2114.8 183.0 %reduce-scatter.11.cloned.1.call-done = f32[128,1024]{1,0:T(8,128)} async-done(((f32[2048,1024]{1,0:T(8,128)}), f32[128,1024]{1,0:T(8,128)}) %reduce-scatter.11.cloned.1.call-update) | async-done | bytes 524304 | tf_op jit(solution)/shard_map/reduce_scatter | solution.py:318
  2297.8 183.1 %reduce-scatter.19.cloned.1.call-done = f32[128,1024]{1,0:T(8,128)} async-done(((f32[2048,1024]{1,0:T(8,128)}), f32[128,1024]{1,0:T(8,128)}) %reduce-scatter.19.cloned.1.call-update) | async-done | bytes 524304 | tf_op jit(solution)/shard_map/reduce_scatter | solution.py:323
  2480.9 183.0 %reduce-scatter.13.cloned.1.call-done = f32[128,1024]{1,0:T(8,128)} async-done(((f32[2048,1024]{1,0:T(8,128)}), f32[128,1024]{1,0:T(8,128)}) %reduce-scatter.13.cloned.1.call-update) | async-done | bytes 524304 | tf_op jit(solution)/shard_map/reduce_scatter | solution.py:319
  2663.9 183.1 %reduce-scatter.15.cloned.1.call-done = f32[128,1024]{1,0:T(8,128)} async-done(((f32[2048,1024]{1,0:T(8,128)}), f32[128,1024]{1,0:T(8,128)}) %reduce-scatter.15.cloned.1.call-update) | async-done | bytes 524304 | tf_op jit(solution)/shard_map/reduce_scatter | solution.py:320
  2847.0 482.0 %reduce-scatter.23.cloned.1.call-done = f32[128,2816]{1,0:T(8,128)} async-done(((f32[2048,2816]{1,0:T(8,128)}), f32[128,2816]{1,0:T(8,128)}) %reduce-scatter.23.cloned.1.call-update) | async-done | bytes 1441808 | tf_op jit(solution)/shard_map/reduce_scatter | solution.py:328
  3329.0 482.7 %reduce-scatter.25.cloned.1.call-done = f32[128,2816]{1,0:T(8,128)} async-done(((f32[2048,2816]{1,0:T(8,128)}), f32[128,2816]{1,0:T(8,128)}) %reduce-scatter.25.cloned.1.call-update) | async-done | bytes 1441808 | tf_op jit(solution)/shard_map/reduce_scatter | solution.py:329
  3811.7 482.5 %reduce-scatter.27.cloned.1.call-done = f32[2816,128]{1,0:T(8,128)} async-done(((f32[2816,2048]{1,0:T(8,128)}), f32[2816,128]{1,0:T(8,128)}) %reduce-scatter.27.cloned.1.call-update) | async-done | bytes 1441808 | tf_op jit(solution)/shard_map/reduce_scatter | solution.py:330
  (580 shorter events, 1024.4 us)
Async XLA Ops:
  7.2 128.0 %all-gather.24.cloned.1.call-start = ((), (), s32[]{:S(2)}) async-start(), calls=%async_computation.10 | async-start | bytes 4456448 | tf_op jit(solution)/shard_map/all_gather | solution.py:160
  7.9 160.8 %all-gather.26.cloned.1.call-start = ((), (), s32[]{:S(2)}) async-start(), calls=%async_computation.11 | async-start | bytes 4456448 | tf_op jit(solution)/shard_map/all_gather | solution.py:161
  8.7 249.8 %all-gather.22.cloned.1.call-start = ((), (), s32[]{:S(2)}) async-start(), calls=%async_computation.9 | async-start | bytes 4456448 | tf_op jit(solution)/shard_map/all_gather | solution.py:159
  9.4 350.9 %all-gather.38.cloned.1.call-start = ((), (), s32[]{:S(2)}) async-start(), calls=%async_computation.28 | async-start | bytes 8912896 | tf_op jit(solution)/shard_map/all_gather | solution.py:13
  148.9 325.7 %all-gather.40.cloned.1.call-start = ((), (), s32[]{:S(2)}) async-start(), calls=%async_computation.29 | async-start | bytes 8912896 | tf_op jit(solution)/shard_map/all_gather | solution.py:13
  175.8 495.4 %all-gather.28.cloned.1.call-start = ((), (), s32[]{:S(2)}) async-start(), calls=%async_computation.12 | async-start | bytes 4456448 | tf_op jit(solution)/shard_map/all_gather | solution.py:164
  176.4 502.7 %all-gather.30.cloned.1.call-start = ((), (), s32[]{:S(2)}) async-start(), calls=%async_computation.13 | async-start | bytes 4456448 | tf_op jit(solution)/shard_map/all_gather | solution.py:165
  177.1 647.1 %all-gather.36.cloned.1.call-start = ((), (), s32[]{:S(2)}) async-start(), calls=%async_computation.17 | async-start | bytes 12255232 | tf_op jit(solution)/shard_map/all_gather | solution.py:171
  177.8 679.2 %all-reduce.12.cloned.1.call-start = ((), (), s32[]{:S(2)}) async-start(), calls=%async_computation.14 | async-start | bytes 8388608 | tf_op jit(solution)/shard_map/psum | solution.py:230
  686.0 315.0 %all-gather.34.cloned.1.call-start = ((), (), s32[]{:S(2)}) async-start(), calls=%async_computation.16 | async-start | bytes 12255232 | tf_op jit(solution)/shard_map/all_gather | solution.py:170
  686.6 458.0 %all-gather.32.cloned.1.call-start = ((), (), s32[]{:S(2)}) async-start(), calls=%async_computation.15 | async-start | bytes 12255232 | tf_op jit(solution)/shard_map/all_gather | solution.py:169
  687.4 517.5 %all-reduce.14.cloned.1.call-start = ((), (), s32[]{:S(2)}) async-start(), calls=%async_computation.18 | async-start | bytes 4194304 | tf_op jit(solution)/shard_map/psum | solution.py:272
  1183.0 490.2 %all-gather.42.cloned.1.call-start = ((), (), s32[]{:S(2)}) async-start(), calls=%async_computation.30 | async-start | bytes 4456448 | tf_op jit(solution)/shard_map/all_gather | solution.py:31
  1596.5 154.1 %all-gather.44.cloned.1.call-start = ((), (), s32[]{:S(2)}) async-start(), calls=%async_computation.31 | async-start | bytes 4456448 | tf_op jit(solution)/shard_map/all_gather | solution.py:31
  1597.1 311.8 %all-reduce.16.cloned.1.call-start = ((), (), s32[]{:S(2)}) async-start(), calls=%async_computation.32 | async-start | bytes 8388608 | tf_op jit(solution)/shard_map/psum | solution.py:238
  1823.9 169.2 %reduce-scatter.17.cloned.1.call-start = ((), (), s32[]{:S(2)}) async-start(), calls=%async_computation.22 | async-start | bytes 1114112 | tf_op jit(solution)/shard_map/reduce_scatter | solution.py:321
  1827.5 287.3 %reduce-scatter.21.cloned.1.call-start = ((), (), s32[]{:S(2)}) async-start(), calls=%async_computation.24 | async-start | bytes 8912896 | tf_op jit(solution)/shard_map/reduce_scatter | solution.py:324
  1835.9 461.9 %reduce-scatter.11.cloned.1.call-start = ((), (), s32[]{:S(2)}) async-start(), calls=%async_computation.19 | async-start | bytes 8912896 | tf_op jit(solution)/shard_map/reduce_scatter | solution.py:318
  1843.0 637.9 %reduce-scatter.19.cloned.1.call-start = ((), (), s32[]{:S(2)}) async-start(), calls=%async_computation.23 | async-start | bytes 8912896 | tf_op jit(solution)/shard_map/reduce_scatter | solution.py:323
  1850.6 813.3 %reduce-scatter.13.cloned.1.call-start = ((), (), s32[]{:S(2)}) async-start(), calls=%async_computation.20 | async-start | bytes 8912896 | tf_op jit(solution)/shard_map/reduce_scatter | solution.py:319
  1857.8 989.2 %reduce-scatter.15.cloned.1.call-start = ((), (), s32[]{:S(2)}) async-start(), calls=%async_computation.21 | async-start | bytes 8912896 | tf_op jit(solution)/shard_map/reduce_scatter | solution.py:320
  1865.0 1464.1 %reduce-scatter.23.cloned.1.call-start = ((), (), s32[]{:S(2)}) async-start(), calls=%async_computation.25 | async-start | bytes 24510464 | tf_op jit(solution)/shard_map/reduce_scatter | solution.py:328
  1878.1 1933.6 %reduce-scatter.25.cloned.1.call-start = ((), (), s32[]{:S(2)}) async-start(), calls=%async_computation.26 | async-start | bytes 24510464 | tf_op jit(solution)/shard_map/reduce_scatter | solution.py:329
  1891.1 2403.1 %reduce-scatter.27.cloned.1.call-start = ((), (), s32[]{:S(2)}) async-start(), calls=%async_computation.27 | async-start | bytes 24510464 | tf_op jit(solution)/shard_map/reduce_scatter | solution.py:330
  (101 other events, 1403.6 us)
Sparse Core Ops, SparseCore 0:
  10.8 76.9 all-gather.23
  90.6 78.1 all-gather.25
  171.5 75.1 all-gather.21
  250.0 110.3 all-gather.37
  363.5 111.0 all-gather.39
  477.2 75.6 all-gather.27
  555.6 85.0 all-gather.29
  643.3 180.8 all-gather.35
  827.3 29.7 all-reduce.11
  860.0 141.0 all-gather.33
  1004.2 140.3 all-gather.31
  1183.1 21.6 all-reduce.13
  1596.6 76.6 all-gather.41
  1675.9 74.6 all-gather.43
  1824.0 27.7 all-reduce.15
  1854.6 67.9 reduce-scatter.16
  1925.3 189.4 reduce-scatter.20
  2117.5 180.1 reduce-scatter.10
  2300.6 180.2 reduce-scatter.18
  2483.6 180.2 reduce-scatter.12
  2666.7 180.2 reduce-scatter.14
  2849.9 479.0 reduce-scatter.22
  3331.9 479.7 reduce-scatter.24
  3814.4 479.7 reduce-scatter.26
where the time goes:
time: 4310 us; the launch traced here: 4300 us
  waiting for transfers between devices  3040 us (71%)
  matrix products  532 us (12%)
  blocking collectives  318 us (7%)
  other arithmetic  246 us (6%)
  local copies, waits for them, and re-layouts  123 us (3%)
    reduce_scatter x1, waiting for transfers between devices, shards(): lax.psum_scatter(up_grad, 'seq', scatter_dimension=0, tiled=True)  483 us
    reduce_scatter x1, waiting for transfers between devices, shards(): lax.psum_scatter(down_grad, 'seq', scatter_dimension=1, tiled=True)  483 us
    reduce_scatter x1, waiting for transfers between devices, shards(): lax.psum_scatter(gate_grad, 'seq', scatter_dimension=0, tiled=True)  482 us
    all_gather x2, waiting for transfers between devices, prefix_2(): everything = jax.tree.map(lambda part: lax.all_gather(part, axis), shard)  200 us
    reduce_scatter x1, waiting for transfers between devices, shards(): lax.psum_scatter(value_grad, 'seq', scatter_dimension=0, tiled=True)  183 us
    reduce_scatter x1, waiting for transfers between devices, shards(): lax.psum_scatter(outgate_grad, 'seq', scatter_dimension=0, tiled=True)  183 us
    reduce_scatter x1, waiting for transfers between devices, shards(): lax.psum_scatter(key_grad, 'seq', scatter_dimension=0, tiled=True)  183 us
    reduce_scatter x1, waiting for transfers between devices, shards(): lax.psum_scatter(query_grad, 'seq', scatter_dimension=0, tiled=True)  183 us
  transfers between devices with their start and end apart: 24, of which 18 were waited for; matrix products, arithmetic and copies ran while one was open for 9% of the time, Pallas kernels for 0%

commit v1 on v0

--- a/solution.py
+++ b/solution.py
@@ -6,6 +6,22 @@
 HIGH = lax.Precision.HIGHEST
 TAU = 8.0
 EPS = 1e-06
+
+
+def ring_gather(x, axis, dim):
+    ways, here, step = (lax.axis_size(axis), lax.axis_index(axis), x.shape[dim])
+    dims = [n * ways if d == dim else n for d, n in enumerate(x.shape)]
+    full = lax.dynamic_update_slice_in_dim(jnp.zeros(dims, x.dtype), x, here * step, axis=dim)
+    going_up = going_down = x
+    for far in range(1, ways // 2 + 1):
+        going_up = lax.ppermute(going_up, axis, [(d, (d + 1) % ways) for d in range(ways)])
+        full = lax.dynamic_update_slice_in_dim(full, going_up, (here - far) % ways * step, axis=dim)
+        if 2 * far < ways:
+            going_down = lax.ppermute(going_down, axis, [(d, (d - 1) % ways) for d in range(ways)])
+            full = lax.dynamic_update_slice_in_dim(
+                full, going_down, (here + far) % ways * step, axis=dim
+            )
+    return full
 
 
 def prefix_2(shard, axis, combine, identity):
@@ -168,7 +184,7 @@
         lax.all_gather(second_gain, "seq", axis=0, tiled=True),
         lax.all_gather(gate_weight, "seq", axis=0, tiled=True),
         lax.all_gather(up_weight, "seq", axis=0, tiled=True),
-        lax.all_gather(down_weight, "seq", axis=1, tiled=True),
+        ring_gather(down_weight, "seq", 1),
     )
     query_full = full[0]
     key_full = full[1]

time: 4310 us -> 4500 us (1.044)
  waiting for transfers between devices: 3040 us -> 3200 us
    ppermute x0 -> x15, waiting for transfers between devices: none -> 233 us  [the longest x8 180 us: ring_gather(): lax.ppermute(going_up, axis, [(d, (d + 1) % ways) for d in range(ways)])]
    all_gather x2, waiting for transfers between devices: 95.1 us -> 0.01 us  [entering(): lax.all_gather(part.astype(kind), axis)]
    reduce_scatter x1, waiting for transfers between devices: 122 us -> 183 us  [shards(): lax.psum_scatter(output_grad, 'seq', scatter_dimension=1, tiled=True)]
    reduce_scatter x1, waiting for transfers between devices: 183 us -> 122 us  [shards(): lax.psum_scatter(query_grad, 'seq', scatter_dimension=0, tiled=True)]
  transfers between devices with their start and end apart: 24 -> 39, of which waited for: 18 -> 28; matrix products, arithmetic and copies ran while one was open for 9% -> 9% of each run, Pallas kernels for 0% -> 0%
where the time goes in v1:
time: 4500 us; the launch traced here: 4490 us
  waiting for transfers between devices  3200 us (71%)
  matrix products  536 us (12%)
  blocking collectives  334 us (7%)
  other arithmetic  235 us (5%)
  local copies, waits for them, and re-layouts  136 us (3%)
    reduce_scatter x1, waiting for transfers between devices, shards(): lax.psum_scatter(up_grad, 'seq', scatter_dimension=0, tiled=True)  483 us
    reduce_scatter x1, waiting for transfers between devices, shards(): lax.psum_scatter(down_grad, 'seq', scatter_dimension=1, tiled=True)  483 us
    reduce_scatter x1, waiting for transfers between devices, shards(): lax.psum_scatter(gate_grad, 'seq', scatter_dimension=0, tiled=True)  482 us
    all_gather x2, waiting for transfers between devices, prefix_2(): everything = jax.tree.map(lambda part: lax.all_gather(part, axis), shard)  202 us
    reduce_scatter x1, waiting for transfers between devices, shards(): lax.psum_scatter(outgate_grad, 'seq', scatter_dimension=0, tiled=True)  183 us
    reduce_scatter x1, waiting for transfers between devices, shards(): lax.psum_scatter(value_grad, 'seq', scatter_dimension=0, tiled=True)  183 us
    reduce_scatter x1, waiting for transfers between devices, shards(): lax.psum_scatter(output_grad, 'seq', scatter_dimension=1, tiled=True)  183 us
    reduce_scatter x1, waiting for transfers between devices, shards(): lax.psum_scatter(key_grad, 'seq', scatter_dimension=0, tiled=True)  183 us
  transfers between devices with their start and end apart: 39, of which 28 were waited for; matrix products, arithmetic and copies ran while one was open for 9% of the time, Pallas kernels for 0%

profile of v1, /device:TPU:10, one launch (start us, length us, event | category | flops | bytes accessed | tf_op | source)
XLA Modules:
  0.0 4486.1 jit_solution(17276694482927609251)
XLA Ops:
  39.4 40.7 all-gather.7
  83.4 39.9 all_gather.82
  212.1 39.1 all-gather.1
  273.0 87.3 %all-gather.38.cloned.1.call-done = f32[32,2,64,512]{3,2,1,0:T(8,128)} async-done(((f32[2,2,64,512]{3,2,1,0:T(8,128)}), f32[32,2,64,512]{3,2,1,0:T(8,128)}) %all-gather.38.cloned.1.call-update) | async-done | bytes 8388624 | tf_op jit(solution)/shard_map/all_gather | solution.py:29
  360.3 114.2 %all-gather.40.cloned.1.call-done = f32[32,2,64,512]{3,2,1,0:T(8,128)} async-done(((f32[2,2,64,512]{3,2,1,0:T(8,128)}), f32[32,2,64,512]{3,2,1,0:T(8,128)}) %all-gather.40.cloned.1.call-update) | async-done | bytes 8388624 | tf_op jit(solution)/shard_map/all_gather | solution.py:29
  501.6 139.9 %while.73 = (s32[]{:T(128)}, f32[2,2,256,512]{2,3,0,1:T(8,128)}, f32[2,2,256,512]{3,2,1,0:T(8,128)}, f32[2,2,256,512]{3,2,1,0:T(8,128)}, f32[2,2,256,64]{2,3,1,0...) while((s32[]{:T(128)}, f32[2,2,256,512]{2,3,0,1:T(8,128)}, ...), condition=%wide.region_10.11_spmd.clone.clone, body=%wide.region_5.10_spmd.clone.clone.sunk | while | flops 2287010304 | bytes 26756780 | solution.py:129
  694.1 130.1 %all-gather.36.cloned.1.call-done = bf16[2816,2048]{1,0:T(8,128)(2,1)} async-done(((bf16[2816,128]{1,0:T(8,128)(2,1)}), bf16[2816,2048]{1,0:T(8,128)(2,1)}) %all-gather.36.cloned.1.call-update) | async-done | bytes 11534352 | tf_op jit(solution)/shard_map/all_gather | solution.py:269
  862.2 138.8 %all-gather.34.cloned.1.call-done = bf16[2048,2816]{1,0:T(8,128)(2,1)} async-done(((bf16[128,2816]{1,0:T(8,128)(2,1)}), bf16[2048,2816]{1,0:T(8,128)(2,1)}) %all-gather.34.cloned.1.call-update) | async-done | bytes 11534352 | tf_op jit(solution)/shard_map/all_gather | solution.py:186
  1012.1 132.4 %all-gather.32.cloned.1.call-done = bf16[2048,2816]{1,0:T(8,128)(2,1)} async-done(((bf16[128,2816]{1,0:T(8,128)(2,1)}), bf16[2048,2816]{1,0:T(8,128)(2,1)}) %all-gather.32.cloned.1.call-update) | async-done | bytes 11534352 | tf_op jit(solution)/shard_map/all_gather | solution.py:185
  1224.0 363.3 %while.72 = (s32[]{:T(128)}, f32[2,2,256,512]{2,3,0,1:T(8,128)}, f32[2,2,256,512]{2,3,0,1:T(8,128)}, f32[2,2,256,512]{2,3,0,1:T(8,128)}, f32[2,2,256,64]{2,3,1,0...) while((s32[]{:T(128)}, f32[2,2,256,512]{2,3,0,1:T(8,128)}, ...), condition=%wide.region_29.30_spmd, body=%wide.region_18.29_spmd.sunk | while | flops 5497390080 | bytes 98163696 | solution.py:129
  1242.0 35.2 fusion.376
  1465.5 35.2 fusion.380
  1625.4 38.0 collective-permute-done.2
  1672.1 39.7 collective-permute-done.4
  1711.8 38.8 all-gather.5
  2089.9 77.7 %all-reduce.6 = (f32[2,64]{1,0:T(2,128)S(1)}, f32[512]{0:T(512)S(1)}, f32[2048]{0:T(1024)S(1)}, f32[2048]{0:T(1024)S(1)}) all-reduce(f32[2,64]{1,0:T(2,128)S(1)} %reshape.331, bf16[512]{0:T(512)(128)(2,1)S(1)} %psum.39, f32[2048]{0:T(1024)S(1)} %get-tuple-element.1070, ...), channel_id=12, replica_groups=mesh['seq'=16,'head'=2] {'seq'}, use_global_device_ids=true, to_apply=%region_43.44.clone | all-reduce | flops 4736 | bytes 36864
  2177.4 121.7 %reduce-scatter.11.cloned.1.call-done = f32[128,1024]{1,0:T(8,128)} async-done(((f32[2048,1024]{1,0:T(8,128)}), f32[128,1024]{1,0:T(8,128)}) %reduce-scatter.11.cloned.1.call-update) | async-done | bytes 524304 | tf_op jit(solution)/shard_map/reduce_scatter | solution.py:334
  2299.1 183.2 %reduce-scatter.19.cloned.1.call-done = f32[128,1024]{1,0:T(8,128)} async-done(((f32[2048,1024]{1,0:T(8,128)}), f32[128,1024]{1,0:T(8,128)}) %reduce-scatter.19.cloned.1.call-update) | async-done | bytes 524304 | tf_op jit(solution)/shard_map/reduce_scatter | solution.py:339
  2482.3 183.1 %reduce-scatter.21.cloned.1.call-done = f32[1024,128]{1,0:T(8,128)} async-done(((f32[1024,2048]{1,0:T(8,128)}), f32[1024,128]{1,0:T(8,128)}) %reduce-scatter.21.cloned.1.call-update) | async-done | bytes 524304 | tf_op jit(solution)/shard_map/reduce_scatter | solution.py:340
  2665.4 183.0 %reduce-scatter.13.cloned.1.call-done = f32[128,1024]{1,0:T(8,128)} async-done(((f32[2048,1024]{1,0:T(8,128)}), f32[128,1024]{1,0:T(8,128)}) %reduce-scatter.13.cloned.1.call-update) | async-done | bytes 524304 | tf_op jit(solution)/shard_map/reduce_scatter | solution.py:335
  2848.4 183.1 %reduce-scatter.15.cloned.1.call-done = f32[128,1024]{1,0:T(8,128)} async-done(((f32[2048,1024]{1,0:T(8,128)}), f32[128,1024]{1,0:T(8,128)}) %reduce-scatter.15.cloned.1.call-update) | async-done | bytes 524304 | tf_op jit(solution)/shard_map/reduce_scatter | solution.py:336
  3031.6 482.0 %reduce-scatter.23.cloned.1.call-done = f32[128,2816]{1,0:T(8,128)} async-done(((f32[2048,2816]{1,0:T(8,128)}), f32[128,2816]{1,0:T(8,128)}) %reduce-scatter.23.cloned.1.call-update) | async-done | bytes 1441808 | tf_op jit(solution)/shard_map/reduce_scatter | solution.py:344
  3513.6 482.7 %reduce-scatter.25.cloned.1.call-done = f32[128,2816]{1,0:T(8,128)} async-done(((f32[2048,2816]{1,0:T(8,128)}), f32[128,2816]{1,0:T(8,128)}) %reduce-scatter.25.cloned.1.call-update) | async-done | bytes 1441808 | tf_op jit(solution)/shard_map/reduce_scatter | solution.py:345
  3996.3 482.5 %reduce-scatter.27.cloned.1.call-done = f32[2816,128]{1,0:T(8,128)} async-done(((f32[2816,2048]{1,0:T(8,128)}), f32[2816,128]{1,0:T(8,128)}) %reduce-scatter.27.cloned.1.call-update) | async-done | bytes 1441808 | tf_op jit(solution)/shard_map/reduce_scatter | solution.py:346
  (679 shorter events, 1217.7 us)
Async XLA Ops:
  7.2 127.4 %all-gather.24.cloned.1.call-start = ((), (), s32[]{:S(2)}) async-start(), calls=%async_computation.10 | async-start | bytes 4456448 | tf_op jit(solution)/shard_map/all_gather | solution.py:176
  7.9 160.8 %all-gather.26.cloned.1.call-start = ((), (), s32[]{:S(2)}) async-start(), calls=%async_computation.11 | async-start | bytes 4456448 | tf_op jit(solution)/shard_map/all_gather | solution.py:177
  8.7 243.2 %all-gather.22.cloned.1.call-start = ((), (), s32[]{:S(2)}) async-start(), calls=%async_computation.9 | async-start | bytes 4456448 | tf_op jit(solution)/shard_map/all_gather | solution.py:175
  9.4 350.9 %all-gather.38.cloned.1.call-start = ((), (), s32[]{:S(2)}) async-start(), calls=%async_computation.28 | async-start | bytes 8912896 | tf_op jit(solution)/shard_map/all_gather | solution.py:29
  148.5 326.0 %all-gather.40.cloned.1.call-start = ((), (), s32[]{:S(2)}) async-start(), calls=%async_computation.29 | async-start | bytes 8912896 | tf_op jit(solution)/shard_map/all_gather | solution.py:29
  175.8 467.6 %all-gather.28.cloned.1.call-start = ((), (), s32[]{:S(2)}) async-start(), calls=%async_computation.12 | async-start | bytes 4456448 | tf_op jit(solution)/shard_map/all_gather | solution.py:180
  176.4 474.6 %all-gather.30.cloned.1.call-start = ((), (), s32[]{:S(2)}) async-start(), calls=%async_computation.13 | async-start | bytes 4456448 | tf_op jit(solution)/shard_map/all_gather | solution.py:181
  177.1 647.0 %all-gather.36.cloned.1.call-start = ((), (), s32[]{:S(2)}) async-start(), calls=%async_computation.17 | async-start | bytes 12255232 | tf_op jit(solution)/shard_map/all_gather | solution.py:269
  177.9 679.1 %all-reduce.12.cloned.1.call-start = ((), (), s32[]{:S(2)}) async-start(), calls=%async_computation.14 | async-start | bytes 8388608 | tf_op jit(solution)/shard_map/psum | solution.py:246
  658.2 342.8 %all-gather.34.cloned.1.call-start = ((), (), s32[]{:S(2)}) async-start(), calls=%async_computation.16 | async-start | bytes 12255232 | tf_op jit(solution)/shard_map/all_gather | solution.py:186
  658.8 485.7 %all-gather.32.cloned.1.call-start = ((), (), s32[]{:S(2)}) async-start(), calls=%async_computation.15 | async-start | bytes 12255232 | tf_op jit(solution)/shard_map/all_gather | solution.py:185
  659.6 541.6 %all-reduce.14.cloned.1.call-start = ((), (), s32[]{:S(2)}) async-start(), calls=%async_computation.18 | async-start | bytes 4194304 | tf_op jit(solution)/shard_map/psum | solution.py:288
  1179.3 746.3 %all-gather.42.cloned.1.call-start = ((), (), s32[]{:S(2)}) async-start(), calls=%async_computation.30 | async-start | bytes 4456448 | tf_op jit(solution)/shard_map/all_gather | solution.py:47
  1587.4 342.9 %all-gather.44.cloned.1.call-start = ((), (), s32[]{:S(2)}) async-start(), calls=%async_computation.31 | async-start | bytes 4456448 | tf_op jit(solution)/shard_map/all_gather | solution.py:47
  1757.7 328.9 %all-reduce.16.cloned.1.call-start = ((), (), s32[]{:S(2)}) async-start(), calls=%async_computation.32 | async-start | bytes 8388608 | tf_op jit(solution)/shard_map/psum | solution.py:254
  2001.2 176.2 %reduce-scatter.17.cloned.1.call-start = ((), (), s32[]{:S(2)}) async-start(), calls=%async_computation.22 | async-start | bytes 1114112 | tf_op jit(solution)/shard_map/reduce_scatter | solution.py:337
  2004.7 294.4 %reduce-scatter.11.cloned.1.call-start = ((), (), s32[]{:S(2)}) async-start(), calls=%async_computation.19 | async-start | bytes 8912896 | tf_op jit(solution)/shard_map/reduce_scatter | solution.py:334
  2010.7 471.6 %reduce-scatter.19.cloned.1.call-start = ((), (), s32[]{:S(2)}) async-start(), calls=%async_computation.23 | async-start | bytes 8912896 | tf_op jit(solution)/shard_map/reduce_scatter | solution.py:339
  2018.6 646.8 %reduce-scatter.21.cloned.1.call-start = ((), (), s32[]{:S(2)}) async-start(), calls=%async_computation.24 | async-start | bytes 8912896 | tf_op jit(solution)/shard_map/reduce_scatter | solution.py:340
  2027.7 820.7 %reduce-scatter.13.cloned.1.call-start = ((), (), s32[]{:S(2)}) async-start(), calls=%async_computation.20 | async-start | bytes 8912896 | tf_op jit(solution)/shard_map/reduce_scatter | solution.py:335
  2035.2 996.3 %reduce-scatter.15.cloned.1.call-start = ((), (), s32[]{:S(2)}) async-start(), calls=%async_computation.21 | async-start | bytes 8912896 | tf_op jit(solution)/shard_map/reduce_scatter | solution.py:336
  2042.3 1471.3 %reduce-scatter.23.cloned.1.call-start = ((), (), s32[]{:S(2)}) async-start(), calls=%async_computation.25 | async-start | bytes 24510464 | tf_op jit(solution)/shard_map/reduce_scatter | solution.py:344
  2055.7 1940.6 %reduce-scatter.25.cloned.1.call-start = ((), (), s32[]{:S(2)}) async-start(), calls=%async_computation.26 | async-start | bytes 24510464 | tf_op jit(solution)/shard_map/reduce_scatter | solution.py:345
  2068.9 2410.0 %reduce-scatter.27.cloned.1.call-start = ((), (), s32[]{:S(2)}) async-start(), calls=%async_computation.27 | async-start | bytes 24510464 | tf_op jit(solution)/shard_map/reduce_scatter | solution.py:346
  (142 other events, 3375.2 us)
Sparse Core Ops, SparseCore 0:
  10.8 76.9 all-gather.23
  90.6 78.1 all-gather.25
  171.5 75.1 all-gather.21
  250.0 110.3 all-gather.37
  363.5 111.0 all-gather.39
  477.2 75.6 all-gather.27
  555.6 84.9 all-gather.29
  643.3 180.7 all-gather.35
  827.2 29.7 all-reduce.11
  859.9 141.0 all-gather.33
  1004.1 140.3 all-gather.31
  1179.4 21.6 all-reduce.13
  1587.5 136.2 all-gather.41
  1757.8 134.9 all-gather.43
  2001.3 34.8 all-reduce.15
  2039.0 67.9 reduce-scatter.16
  2109.6 189.4 reduce-scatter.10
  2301.8 180.4 reduce-scatter.18
  2485.2 180.2 reduce-scatter.20
  2668.1 180.2 reduce-scatter.12
  2851.3 180.2 reduce-scatter.14
  3034.4 479.1 reduce-scatter.22
  3516.5 479.7 reduce-scatter.24
  3999.0 479.7 reduce-scatter.26
